TPU v7x, 32 devices: a whole 2x2x4 slice. The times are simulated.
32 devices in a mesh: row: 8 (over z, x), col: 4 (over y, core).
Axes of the slice: x: 2, y: 2, z: 4, core: 2. Of those that a mesh axis runs over, the one named last changes fastest.
Arguments:
- panels_t: float32 [1024, 2048], P('col', 'row'), as said below
- trailing_t: float32 [3072, 2048], P('col', 'row'), may hold values from -0.125 to 0.125
Outputs:
- r_factor: float32 [1024, 1024], P('row', 'col')
- coefficients: float32 [1024, 3072], P('row', 'col')
Inputs may be any that keep to these rules, and one draw needn't show every extreme that they name: `panels_t`: panel_matrix has full column rank.
All inputs are finite; a program needn't handle non-finite values.
Results may differ from a plain program's by a relative error of at most 0.0003.
Values sent between devices are 32-bit elements; how exact they have to be, the bound alone decides.
A program may use at most 64 MiB of HBM per device.

v0:
```python
import jax
import jax.numpy as jnp
from jax import lax
from jax.sharding import PartitionSpec as P


def product(left, right):
    return jnp.dot(left, right, precision=lax.Precision.HIGHEST)


def factor_pair(gram):
    lower_f = jnp.linalg.cholesky(gram)
    identity = jnp.eye(gram.shape[0], dtype=gram.dtype)
    inverse = jax.scipy.linalg.solve_triangular(lower_f, identity, lower=True)
    return (lower_f, inverse)


def local(panels_t, trailing_t):
    panel = lax.all_gather(panels_t, "col", axis=0, tiled=True)
    width = panel.shape[0] // 2
    first_panel = panel[:width]
    second_panel = panel[width:]
    gram_one, gram_cross, gram_two, cross_block = lax.psum(
        (
            product(first_panel, first_panel.T),
            product(first_panel, second_panel.T),
            product(second_panel, second_panel.T),
            product(panel, trailing_t.T),
        ),
        "row",
    )
    lower_one, invert_one = factor_pair(gram_one)
    upper_right = product(invert_one, gram_cross)
    lower_two, invert_two = factor_pair(gram_two - product(upper_right.T, upper_right))
    top_one = product(invert_one, cross_block[:width])
    top_two = product(invert_two, cross_block[width:] - product(upper_right.T, top_one))
    zeros_left = jnp.zeros((width, width), jnp.float32)
    upper_rows = jnp.concatenate([lower_one.T, upper_right], axis=1)
    lower_rows = jnp.concatenate([zeros_left, lower_two.T], axis=1)
    r_full = jnp.concatenate([upper_rows, lower_rows], axis=0)
    lower_solution = product(invert_two.T, top_two)
    upper_solution = product(invert_one.T, top_one - product(upper_right, lower_solution))
    solution = jnp.concatenate([upper_solution, lower_solution], axis=0)
    total = r_full.shape[0]
    rows_out = total // lax.axis_size("row")
    cols_out = total // lax.axis_size("col")
    row_start = lax.axis_index("row") * rows_out
    col_start = lax.axis_index("col") * cols_out
    r_block = lax.dynamic_slice(r_full, (row_start, col_start), (rows_out, cols_out))
    coef_block = lax.dynamic_slice_in_dim(solution, row_start, rows_out, 0)
    return (r_block, coef_block)


def solution(mesh):
    placed = (P("col", "row"), P("col", "row"))
    return jax.shard_map(
        local,
        mesh=mesh,
        in_specs=placed,
        out_specs=(P("row", "col"), P("row", "col")),
        check_vma=False,
    )
```

profile of v0, /device:TPU:0, one launch (start us, length us, event | category | flops | bytes accessed | tf_op | source)
XLA Modules:
  0.0 594.6 jit_solution(517147692076575606)
XLA Ops:
  8.0 21.0 %all-gather.2.cloned.1.call-done = f32[1024,256]{1,0:T(8,128)} async-done(((f32[256,256]{1,0:T(8,128)}), f32[1024,256]{1,0:T(8,128)}) %all-gather.2.cloned.1.call-update) | async-done | bytes 1048592 | tf_op jit(solution)/shard_map/all_gather | solution.py:19
  29.0 3.3 fusion.29
  36.4 4.4 fusion.90
  41.0 210.4 %all-reduce.5.cloned.1.call-done = (f32[512,512]{0,1:T(8,128)}, f32[512,512]{1,0:T(8,128)}, f32[512,512]{0,1:T(8,128)}, f32[1024,768]{1,0:T(8,128)}) async-done(((f32[512,512]{0,1:T(8,128)}, f32[512,512]{1,0:T(8,128)}, f32[512,512]{0,1:T(8,128)}, f32[1024,768]{1,0:T(8,128)}), (f32[512,512]{0,1:T(8,128)}, f32[512,512]{1,0:T(8,128)}, f32[512,512]{0,1:T(8,128)}, ...) | async-done | bytes 6291472 | tf_op jit(solution)/shard_map/psum | solution.py:23
  256.5 11.7 %cholesky.286 = f32[128,128]{1,0:T(8,128)S(1)} custom-call(f32[128,128]{1,0:T(8,128)S(1)} %cholesky.426), custom_call_target="Cholesky" | custom-call | tf_op jit(solution)/shard_map/jit(cholesky)/cholesky | solution.py:12
  268.4 10.0 %custom-call.27 = f32[1,128,128]{1,2,0:T(8,128)S(1)} custom-call(f32[1,128,128]{2,1,0:T(8,128)S(1)} %get-tuple-element.69), custom_call_target="InvertDiagBlocksLowerTriangular" | custom-call | tf_op jit(solution)/shard_map/jit(cholesky)/cholesky | solution.py:12
  280.9 11.7 %cholesky.305 = f32[128,128]{1,0:T(8,128)S(1)} custom-call(f32[128,128]{1,0:T(8,128)S(1)} %cholesky.430), custom_call_target="Cholesky" | custom-call | tf_op jit(solution)/shard_map/jit(cholesky)/cholesky | solution.py:12
  292.6 9.8 %custom-call.28 = f32[1,128,128]{1,2,0:T(8,128)S(1)} custom-call(f32[1,128,128]{2,1,0:T(8,128)S(1)} %get-tuple-element.66), custom_call_target="InvertDiagBlocksLowerTriangular" | custom-call | tf_op jit(solution)/shard_map/jit(cholesky)/cholesky | solution.py:12
  304.0 11.7 %cholesky.326 = f32[128,128]{1,0:T(8,128)S(1)} custom-call(f32[128,128]{1,0:T(8,128)S(1)} %cholesky.435), custom_call_target="Cholesky" | custom-call | tf_op jit(solution)/shard_map/jit(cholesky)/cholesky | solution.py:12
  315.8 10.2 %custom-call.29 = f32[1,128,128]{1,2,0:T(8,128)S(1)} custom-call(f32[1,128,128]{2,1,0:T(8,128)S(1)} %get-tuple-element.63), custom_call_target="InvertDiagBlocksLowerTriangular" | custom-call | tf_op jit(solution)/shard_map/jit(cholesky)/cholesky | solution.py:12
  327.4 11.7 %cholesky.343 = f32[128,128]{1,0:T(8,128)S(1)} custom-call(f32[128,128]{1,0:T(8,128)S(1)} %convolution_subtract_fusion.12), custom_call_target="Cholesky" | custom-call | tf_op jit(solution)/shard_map/jit(cholesky)/cholesky | solution.py:12
  345.3 11.6 %while.4 = (s32[]{:T(128)}, f32[512,512]{1,0:T(8,128)}, s32[4,2]{0,1:T(2,128)S(1)}, f32[4,128,128]{2,1,0:T(8,128)S(1)}, s32[]{:T(128)}) while((s32[]{:T(128)}, f32[512,512]{1,0:T(8,128)}, s32[4,2]{0,1:T(2,128)S(1)}, f32[4,128,128]{2,1,0:T(8,128)S(1)}, s32[]{:T(128)}) %tuple.57), condition=%wide.while_cond, body=%wide.while_body.sunk | while | flops 2 | bytes 131189 | solution.py:14
  356.9 39.5 %custom-call.30 = f32[4,128,128]{1,2,0:T(8,128)S(1)} custom-call(f32[4,128,128]{2,1,0:T(8,128)S(1)} %get-tuple-element.18), custom_call_target="InvertDiagBlocksLowerTriangular" | custom-call | tf_op jit(solution)/shard_map/jit(_solve_triangular)/triangular_solve | solution.py:14
  410.2 11.7 %cholesky.358 = f32[128,128]{1,0:T(8,128)S(1)} custom-call(f32[128,128]{1,0:T(8,128)S(1)} %cholesky.439), custom_call_target="Cholesky" | custom-call | tf_op jit(solution)/shard_map/jit(cholesky)/cholesky | solution.py:12
  421.9 10.2 %custom-call.31 = f32[1,128,128]{1,2,0:T(8,128)S(1)} custom-call(f32[1,128,128]{2,1,0:T(8,128)S(1)} %get-tuple-element.59), custom_call_target="InvertDiagBlocksLowerTriangular" | custom-call | tf_op jit(solution)/shard_map/jit(cholesky)/cholesky | solution.py:12
  435.0 11.7 %cholesky.377 = f32[128,128]{1,0:T(8,128)S(1)} custom-call(f32[128,128]{1,0:T(8,128)S(1)} %cholesky.443), custom_call_target="Cholesky" | custom-call | tf_op jit(solution)/shard_map/jit(cholesky)/cholesky | solution.py:12
  446.9 9.8 %custom-call.32 = f32[1,128,128]{1,2,0:T(8,128)S(1)} custom-call(f32[1,128,128]{2,1,0:T(8,128)S(1)} %get-tuple-element.56), custom_call_target="InvertDiagBlocksLowerTriangular" | custom-call | tf_op jit(solution)/shard_map/jit(cholesky)/cholesky | solution.py:12
  458.3 11.9 %cholesky.398 = f32[128,128]{1,0:T(8,128)S(1)} custom-call(f32[128,128]{1,0:T(8,128)S(1)} %cholesky.448), custom_call_target="Cholesky" | custom-call | tf_op jit(solution)/shard_map/jit(cholesky)/cholesky | solution.py:12
  470.2 9.8 %custom-call.33 = f32[1,128,128]{1,2,0:T(8,128)S(1)} custom-call(f32[1,128,128]{2,1,0:T(8,128)S(1)} %get-tuple-element.53), custom_call_target="InvertDiagBlocksLowerTriangular" | custom-call | tf_op jit(solution)/shard_map/jit(cholesky)/cholesky | solution.py:12
  481.5 11.7 %cholesky.415 = f32[128,128]{1,0:T(8,128)S(1)} custom-call(f32[128,128]{1,0:T(8,128)S(1)} %convolution_subtract_fusion.11), custom_call_target="Cholesky" | custom-call | tf_op jit(solution)/shard_map/jit(cholesky)/cholesky | solution.py:12
  500.6 4.4 fusion.1
  505.1 3.8 fusion.91
  509.6 14.2 %while.5 = (s32[]{:T(128)}, f32[512,512]{1,0:T(8,128)}, s32[4,2]{0,1:T(2,128)S(1)}, f32[4,128,128]{2,1,0:T(8,128)}, s32[]{:T(128)}) while((s32[]{:T(128)}, f32[512,512]{1,0:T(8,128)}, s32[4,2]{0,1:T(2,128)S(1)}, f32[4,128,128]{2,1,0:T(8,128)}, s32[]{:T(128)}) %tuple.68), condition=%wide.while_cond.clone, body=%wide.while_body.clone.sunk | while | flops 2 | bytes 132205 | solution.py:14
  523.9 40.9 %custom-call.34 = f32[4,128,128]{1,2,0:T(8,128)} custom-call(f32[4,128,128]{2,1,0:T(8,128)} %get-tuple-element.19), custom_call_target="InvertDiagBlocksLowerTriangular" | custom-call | tf_op jit(solution)/shard_map/jit(_solve_triangular)/triangular_solve | solution.py:14
  (141 shorter events, 92.9 us)
Async XLA Ops:
  7.2 29.3 %copy-start = (f32[768,256]{1,0:T(8,128)S(1)}, f32[768,256]{1,0:T(8,128)}, u32[]{:S(2)}) copy-start(f32[768,256]{1,0:T(8,128)} %param.6) | copy-start | bytes 2359300
  7.2 21.8 %all-gather.2.cloned.1.call-start = ((), (), s32[]{:S(2)}) async-start(), calls=%async_computation | async-start | bytes 1310720 | tf_op jit(solution)/shard_map/all_gather | solution.py:19
  7.9 243.5 %all-reduce.5.cloned.1.call-start = ((), (), s32[]{:S(2)}) async-start(), calls=%async_computation.1 | async-start | bytes 12582912 | tf_op jit(solution)/shard_map/psum | solution.py:23
  29.0 3.3 copy-start.3
  41.0 359.4 %copy-start.6 = (f32[512,512]{1,0:T(8,128)}, f32[512,512]{1,0:T(8,128)S(1)}, u32[]{:S(2)}) copy-start(f32[512,512]{1,0:T(8,128)S(1)} %fusion.9) | copy-start | bytes 3145732
  251.4 2.6 copy-start.13
  255.5 1.0 copy-start.16
  396.8 5.7 copy-start.1
  398.5 4.0 copy-start.4
  400.0 2.6 copy-start.18
  400.4 4.1 copy-start.8
  402.5 2.0 copy-start.11
  402.6 2.0 copy-start.19
  409.2 1.0 copy-start.17
  498.4 1.3 copy-start.14
  564.8 4.3 copy-start.7
  566.3 8.4 %copy-start.15 = (f32[1024,768]{1,0:T(8,128)S(1)}, f32[1024,768]{1,0:T(8,128)}, u32[]{:S(2)}) copy-start(f32[1024,768]{1,0:T(8,128)} %get-tuple-element.41) | copy-start | bytes 9437188
  570.4 4.2 copy-start.10
  580.5 2.9 copy-start.2
  580.5 2.9 copy-start.5
  580.5 2.9 copy-start.9
  580.5 2.9 copy-start.12
Sparse Core Ops, SparseCore 0:
  9.5 19.4 all-gather.1
  41.0 210.3 all-reduce.4
where the time goes:
time: 604 us; the launch traced here: 595 us
  other arithmetic  246 us (41%)
  waiting for transfers between devices  232 us (38%)
  matrix products  62.6 us (10%)
  local copies, waits for them, and re-layouts  33.7 us (6%)
  between operations  20.2 us (3%)
    psum x1, waiting for transfers between devices, local(): lax.psum((product(first_panel, first_panel.T), product(first_panel, secon...  210 us
    another operation x29, other arithmetic, factor_pair(): lower_f = jnp.linalg.cholesky(gram)  159 us
    another operation x4, other arithmetic, factor_pair(): inverse = jax.scipy.linalg.solve_triangular(lower_f, identity, lower=True)  81.7 us
    dot_general x12, matrix products, product(): return jnp.dot(left, right, precision=lax.Precision.HIGHEST)  35.7 us
    another operation x27, local copies, waits for them, and re-layouts, factor_pair(): inverse = jax.scipy.linalg.solve_triangular(lower_f, identity, lower=True)  26.5 us
    all_gather x1, waiting for transfers between devices, local(): panel = lax.all_gather(panels_t, 'col', axis=0, tiled=True)  21 us
    another operation x14, matrix products, factor_pair(): inverse = jax.scipy.linalg.solve_triangular(lower_f, identity, lower=True)  15.8 us
  transfers between devices with their start and end apart: 2, of which 2 were waited for; matrix products, arithmetic and copies ran while one was open for 0% of the time, Pallas kernels for 0%

commit v1 on v0

v1 whole, which is shorter than its diff:
```python
import jax
import jax.numpy as jnp
from jax import lax
from jax.experimental import pallas as pl
from jax.experimental.pallas import tpu as pltpu
from jax.sharding import PartitionSpec as P

BLOCK = 128
MICRO = 8


def product(left, right):
    return jnp.dot(left, right, precision=lax.Precision.HIGHEST)


def lanes(tile, lane):
    return jnp.broadcast_to(tile[:, lane : lane + 1], tile.shape)


def sublanes(tile, row):
    return jnp.broadcast_to(tile[row : row + 1, :], tile.shape)


def factor_block(square):
    count = BLOCK // MICRO
    shape = (MICRO, BLOCK)
    row_id = lax.broadcasted_iota(jnp.int32, shape, 0)
    lane_id = lax.broadcasted_iota(jnp.int32, shape, 1)
    rest = [square[MICRO * i : MICRO * (i + 1), :] for i in range(count)]
    unit = [jnp.where(row_id + MICRO * i == lane_id, 1.0, 0.0) for i in range(count)]
    upper, inverse = [], []
    for b in range(count):
        base = MICRO * b
        tile, side = rest[b], unit[b]
        cols = [lanes(tile, base + c) for c in range(MICRO)]
        scales, pivots, rows, sides = [], {}, [], []
        upper_tile, side_tile = jnp.zeros(shape, jnp.float32), jnp.zeros(shape, jnp.float32)
        for k in range(MICRO):
            scale = lax.rsqrt(sublanes(cols[k], k))
            below = cols[k] * scale
            row = sublanes(tile, k) * scale
            side_row = sublanes(side, k) * scale
            for c in range(k + 1, MICRO):
                pivots[c, k] = sublanes(below, c)
                cols[c] = cols[c] - below * pivots[c, k]
            tile = tile - below * row
            side = side - below * side_row
            upper_tile = jnp.where(row_id == k, row, upper_tile)
            side_tile = jnp.where(row_id == k, side_row, side_tile)
            scales.append(scale)
            rows.append(row)
            sides.append(side_row)
        upper.append(jnp.where(row_id + base <= lane_id, upper_tile, 0.0))
        inverse.append(jnp.where(row_id + base >= lane_id, side_tile, 0.0))
        for i in range(b + 1, count):
            tile, side = rest[i], unit[i]
            cols = [lanes(tile, base + c) for c in range(MICRO)]
            for k in range(MICRO):
                below = cols[k] * scales[k]
                for c in range(k + 1, MICRO):
                    cols[c] = cols[c] - below * pivots[c, k]
                tile = tile - below * rows[k]
                side = side - below * sides[k]
            rest[i], unit[i] = tile, side
    return jnp.concatenate(upper, axis=0), jnp.concatenate(inverse, axis=0)


def factor_kernel(gram_ref, upper_ref, inverse_ref, work_ref):
    total = gram_ref.shape[0]
    work_ref[...] = gram_ref[...]
    column = lax.broadcasted_iota(jnp.int32, (BLOCK, total), 1)

    @pl.loop(0, total // BLOCK)
    def _(k):
        start = pl.multiple_of(k * BLOCK, BLOCK)
        here = pl.ds(start, BLOCK)
        diagonal, inverse = factor_block(work_ref[here, here])
        panel = product(inverse, work_ref[here, :])
        work_ref[here, :] = panel
        work_ref[here, here] = inverse
        upper_ref[here, :] = jnp.where(column >= start + BLOCK, panel, 0.0)
        upper_ref[here, here] = diagonal
        inverse_ref[here, :] = jnp.where(column < start, panel, 0.0)
        inverse_ref[here, here] = inverse

        @pl.loop(k + 1, total // BLOCK)
        def _(i):
            there = pl.ds(pl.multiple_of(i * BLOCK, BLOCK), BLOCK)
            work_ref[there, here] = jnp.zeros((BLOCK, BLOCK), jnp.float32)
            work_ref[there, :] -= lax.dot_general(
                work_ref[here, there],
                work_ref[here, :],
                (((0,), (0,)), ((), ())),
                precision=lax.Precision.HIGHEST,
                preferred_element_type=jnp.float32,
            )


def factor(gram):
    total = gram.shape[0]
    whole = jax.ShapeDtypeStruct(gram.shape, jnp.float32)
    return pl.pallas_call(
        factor_kernel,
        out_shape=(whole, whole),
        in_specs=[pl.BlockSpec(memory_space=pltpu.VMEM)],
        out_specs=(pl.BlockSpec(memory_space=pltpu.VMEM),) * 2,
        scratch_shapes=[pltpu.VMEM(gram.shape, jnp.float32)],
        compiler_params=pltpu.CompilerParams(vmem_limit_bytes=32 * 1024 * 1024),
        cost_estimate=pl.CostEstimate(flops=60 * total**3, bytes_accessed=12 * total**2, transcendentals=0),
    )(gram)


def local(panels_t, trailing_t):
    panel = lax.all_gather(panels_t, "col", axis=0, tiled=True)
    gram_part = lax.psum_scatter(product(panels_t, panel.T), "row", scatter_dimension=0, tiled=True)
    gram = lax.all_gather(gram_part, ("col", "row"), axis=0, tiled=True)
    cross = lax.psum_scatter(product(trailing_t, panel.T), "row", scatter_dimension=0, tiled=True)
    r_full, invert = factor(gram)
    slab = product(product(cross, invert.T), invert)
    spread = lax.all_to_all(slab, "row", split_axis=1, concat_axis=0, tiled=True)
    total = r_full.shape[0]
    rows_out = total // lax.axis_size("row")
    cols_out = total // lax.axis_size("col")
    row_start = lax.axis_index("row") * rows_out
    col_start = lax.axis_index("col") * cols_out
    r_block = lax.dynamic_slice(r_full, (row_start, col_start), (rows_out, cols_out))
    return (r_block, spread.T)


def solution(mesh):
    placed = (P("col", "row"), P("col", "row"))
    return jax.shard_map(
        local,
        mesh=mesh,
        in_specs=placed,
        out_specs=(P("row", "col"), P("row", "col")),
        check_vma=False,
    )
```

time: 604 us -> 270 us (0.45); the launches traced: 595 us -> 270 us
  other arithmetic: 246 us -> 0 us
  waiting for transfers between devices: 232 us -> 171 us
  Pallas kernels: 0 us -> 54.9 us
  matrix products: 62.6 us -> 16.9 us
  local copies, waits for them, and re-layouts: 33.7 us -> 9.37 us
  between operations: 20.2 us -> 13.8 us
    another operation x33 -> x0, other arithmetic: 240 us -> none  [the longest x29 159 us: factor_pair(): lower_f = jnp.linalg.cholesky(gram)]
    psum x1 -> x0, waiting for transfers between devices: 210 us -> none  [local(): lax.psum((product(first_panel, first_panel.T), product(first_panel, secon...]
    reduce_scatter x0 -> x2, waiting for transfers between devices: none -> 80 us  [the longest x1 64.3 us: local(): lax.psum_scatter(product(panels_t, panel.T), 'row', scatter_dimension=0,...]
    all_gather x0 -> x1, waiting for transfers between devices: none -> 59.1 us  [local(): gram = lax.all_gather(gram_part, ('col', 'row'), axis=0, tiled=True)]
    pallas_call x0 -> x1, Pallas kernels: none -> 54.9 us  [factor(): pl.pallas_call(factor_kernel, out_shape=(whole, whole), in_specs=[pl.Bloc...]
    another operation x26 -> x0, matrix products: 27 us -> none  [the longest x14 15.8 us: factor_pair(): inverse = jax.scipy.linalg.solve_triangular(lower_f, identity, lower=True)]
    another operation x37 -> x0, local copies, waits for them, and re-layouts: 26.9 us -> none  [the longest x27 26.5 us: factor_pair(): inverse = jax.scipy.linalg.solve_triangular(lower_f, identity, lower=True)]
    dot_general x12 -> x4, matrix products: 35.7 us -> 16.9 us  [product(): return jnp.dot(left, right, precision=lax.Precision.HIGHEST)]
  transfers between devices with their start and end apart: 2 -> 5, of which waited for: 2 -> 5; matrix products, arithmetic and copies ran while one was open for 0% -> 2% of each run, Pallas kernels for 0% -> 20%
where the time goes in v1:
time: 270 us
  waiting for transfers between devices  171 us (63%)
  Pallas kernels  54.9 us (20%)
  matrix products  16.9 us (6%)
  between operations  13.8 us (5%)
  local copies, waits for them, and re-layouts  9.37 us (3%)
  starting transfers between devices  3.83 us (1%)
    reduce_scatter x1, waiting for transfers between devices, local(): lax.psum_scatter(product(panels_t, panel.T), 'row', scatter_dimension=0,...  64.3 us
    all_gather x1, waiting for transfers between devices, local(): gram = lax.all_gather(gram_part, ('col', 'row'), axis=0, tiled=True)  59.1 us
    pallas_call x1, Pallas kernels, factor(): pl.pallas_call(factor_kernel, out_shape=(whole, whole), in_specs=[pl.Bloc...  54.9 us
    all_gather x1, waiting for transfers between devices, local(): panel = lax.all_gather(panels_t, 'col', axis=0, tiled=True)  21 us
    dot_general x4, matrix products, product(): return jnp.dot(left, right, precision=lax.Precision.HIGHEST)  16.9 us
    reduce_scatter x1, waiting for transfers between devices, local(): lax.psum_scatter(product(trailing_t, panel.T), 'row', scatter_dimension=0...  15.7 us
    all_to_all x1, waiting for transfers between devices, local(): lax.all_to_all(slab, 'row', split_axis=1, concat_axis=0, tiled=True)  9.88 us
    unnamed x13, local copies, waits for them, and re-layouts  7.03 us
  transfers between devices with their start and end apart: 5, of which 5 were waited for; matrix products, arithmetic and copies ran while one was open for 2% of the time, Pallas kernels for 20%

profile of v1, /device:TPU:0, one launch (start us, length us, event | category | flops | bytes accessed | tf_op | source)
XLA Modules:
  0.0 269.6 jit_solution(374531018703529766)
XLA Ops:
  7.2 0.0 all-gather.3.cloned.1.call-start
  7.2 0.7 all-gather.3.cloned.1.call-update
  7.9 0.0 reduce-scatter.3.cloned.1.call-start
  8.0 21.0 %all-gather.3.cloned.1.call-done = f32[1024,256]{1,0:T(8,128)} async-done(((f32[256,256]{1,0:T(8,128)}), f32[1024,256]{1,0:T(8,128)}) %all-gather.3.cloned.1.call-update) | async-done | bytes 1048592 | tf_op jit(solution)/shard_map/all_gather | solution.py:114
  29.0 3.4 %fusion = f32[256,1024]{1,0:T(8,128)} fusion(f32[256,256]{1,0:T(8,128)} %param.2, f32[1024,256]{1,0:T(8,128)} %all-gather.3.cloned.1.call-done), kind=kOutput, calls=%fused_computation.2 | convolution fusion | flops 805306368 | bytes 2359296 | tf_op jit(solution)/shard_map/dot_general | solution.py:13
  32.4 0.0 reduce-scatter.3.cloned.1.call-update
  32.4 0.0 all-gather.5.cloned.1.call-start
  32.5 64.3 %reduce-scatter.3.cloned.1.call-done = f32[32,1024]{1,0:T(8,128)} async-done(((f32[256,1024]{1,0:T(8,128)}), f32[32,1024]{1,0:T(8,128)}) %reduce-scatter.3.cloned.1.call-update) | async-done | bytes 131088 | tf_op jit(solution)/shard_map/reduce_scatter | solution.py:115
  96.8 0.0 all-gather.5.cloned.1.call-update
  96.8 0.0 reduce-scatter.5.cloned.1.call-start
  96.9 4.4 %fusion.1 = f32[768,1024]{1,0:T(8,128)} fusion(f32[768,256]{1,0:T(8,128)S(1)} %copy-done, f32[1024,256]{1,0:T(8,128)S(1)} %copy-done.5), kind=kOutput, calls=%fused_computation.3 | convolution fusion | flops 2415919104 | bytes 4980736 | tf_op jit(solution)/shard_map/dot_general | solution.py:13
  101.3 59.1 %all-gather.5.cloned.1.call-done.gram_ref = f32[1024,1024]{1,0:T(8,128)} async-done(((f32[32,1024]{1,0:T(8,128)}), f32[1024,1024]{1,0:T(8,128)}) %all-gather.5.cloned.1.call-update) | async-done | bytes 4194320 | tf_op jit(solution)/shard_map/all_gather | solution.py:116
  160.4 2.2 copy-done.4
  162.6 54.9 %shard_map.41 = (f32[1024,1024]{1,0:T(8,128)S(1)}, f32[1024,1024]{1,0:T(8,128)S(1)}) custom-call(f32[1024,1024]{1,0:T(8,128)S(1)} %copy-done.4), custom_call_target="tpu_custom_call" | custom-call | flops 64424509440 | bytes 12582912 | tf_op jit(solution)/shard_map/pallas_call | solution.py:102
  217.5 2.0 copy-done.1
  219.5 2.0 copy-done.3
  221.4 15.7 %reduce-scatter.5.cloned.1.call-done = f32[96,1024]{1,0:T(8,128)} async-done(((f32[768,1024]{1,0:T(8,128)}), f32[96,1024]{1,0:T(8,128)}) %reduce-scatter.5.cloned.1.call-update) | async-done | bytes 393232 | tf_op jit(solution)/shard_map/reduce_scatter | solution.py:117
  237.1 6.6 %fusion.2 = f32[96,1024]{1,0:T(8,128)S(1)} fusion(f32[96,1024]{1,0:T(8,128)} %reduce-scatter.5.cloned.1.call-done, f32[1024,1024]{1,0:T(8,128)} %copy-done.1), kind=kOutput, calls=%fused_computation.4 | convolution fusion | flops 1207959552 | bytes 4980736 | tf_op jit(solution)/shard_map/dot_general | solution.py:13
  243.7 2.6 convolution_bitcast_fusion
  246.3 0.8 copy.9
  247.1 3.7 %all-to-all-start = ((f32[96,8,128]{2,0,1:T(8,128)}), f32[96,8,128]{2,0,1:T(8,128)S(1)}, u32[]{:S(2)}, u32[]{:S(2)}) async-start(f32[96,8,128]{2,0,1:T(8,128)} %bitcast.17), calls=%async_computation.2 | async-start | bytes 786432 | tf_op jit(solution)/shard_map/all_to_all | solution.py:120
  250.7 1.6 dynamic_slice.3
  252.3 9.9 %all-to-all-done = f32[96,8,128]{2,0,1:T(8,128)S(1)} async-done(((f32[96,8,128]{2,0,1:T(8,128)}), f32[96,8,128]{2,0,1:T(8,128)S(1)}, u32[]{:S(2)}, u32[]{:S(2)}) %all-to-all-start) | async-done | bytes 393248 | tf_op jit(solution)/shard_map/all_to_all | solution.py:120
  262.2 0.9 copy.6
  (10 shorter events, 0.0 us)
Async XLA Ops:
  7.2 89.7 %copy-start = (f32[768,256]{1,0:T(8,128)S(1)}, f32[768,256]{1,0:T(8,128)}, u32[]{:S(2)}) copy-start(f32[768,256]{1,0:T(8,128)} %param.3) | copy-start | bytes 2359300
  7.2 21.8 %all-gather.3.cloned.1.call-start = ((), (), s32[]{:S(2)}) async-start(), calls=%async_computation.3 | async-start | bytes 1310720 | tf_op jit(solution)/shard_map/all_gather | solution.py:114
  7.9 88.9 %reduce-scatter.3.cloned.1.call-start = ((), (), s32[]{:S(2)}) async-start(), calls=%async_computation.4 | async-start | bytes 1179648 | tf_op jit(solution)/shard_map/reduce_scatter | solution.py:115
  29.0 67.9 %copy-start.5 = (f32[1024,256]{1,0:T(8,128)S(1)}, f32[1024,256]{1,0:T(8,128)}, u32[]{:S(2)}) copy-start(f32[1024,256]{1,0:T(8,128)} %all-gather.3.cloned.1.call-done) | copy-start | bytes 3145732
  32.4 128.0 %all-gather.5.cloned.1.call-start = ((), (), s32[]{:S(2)}) async-start(), calls=%async_computation.5 | async-start | bytes 4325376 | tf_op jit(solution)/shard_map/all_gather | solution.py:116
  96.8 140.3 %reduce-scatter.5.cloned.1.call-start = ((), (), s32[]{:S(2)}) async-start(), calls=%async_computation.6 | async-start | bytes 3538944 | tf_op jit(solution)/shard_map/reduce_scatter | solution.py:117
  160.4 2.2 copy-start.4
  217.5 2.0 copy-start.1
  219.5 2.0 copy-start.3
  237.1 6.6 %copy-start.2 = (f32[1024,1024]{1,0:T(8,128)S(1)}, f32[1024,1024]{1,0:T(8,128)}, u32[]{:S(2)}) copy-start(f32[1024,1024]{1,0:T(8,128)} %copy-done.1) | copy-start | bytes 12582916
  247.1 15.1 %all-to-all-start = ((f32[96,8,128]{2,0,1:T(8,128)}), f32[96,8,128]{2,0,1:T(8,128)S(1)}, u32[]{:S(2)}, u32[]{:S(2)}) async-start(f32[96,8,128]{2,0,1:T(8,128)} %bitcast.17), calls=%async_computation.2 | async-start | bytes 786432 | tf_op jit(solution)/shard_map/all_to_all | solution.py:120
Sparse Core Ops, SparseCore 0:
  9.5 19.4 all-gather.2
  32.6 64.2 reduce-scatter.2
  99.8 60.5 all-gather.4
  163.9 73.2 reduce-scatter.4

commit v2 on v1

--- a/solution.py
+++ b/solution.py
@@ -7,6 +7,7 @@
 
 BLOCK = 128
 MICRO = 8
+MESH = pl.DeviceIdType.MESH
 
 
 def product(left, right):
@@ -65,9 +66,25 @@
     return jnp.concatenate(upper, axis=0), jnp.concatenate(inverse, axis=0)
 
 
-def factor_kernel(gram_ref, upper_ref, inverse_ref, work_ref):
+def unstack(stacked_ref, work_ref, width):
+    count = stacked_ref.shape[0] // width
+    for i in range(count):
+        for j in range(i, count):
+            if j - i <= count // 2:
+                held = stacked_ref[pl.ds(i * width, width), pl.ds((j - i) * width, width)]
+            else:
+                held = stacked_ref[pl.ds(j * width, width), pl.ds((count + i - j) * width, width)].T
+            work_ref[pl.ds(i * width, width), pl.ds(j * width, width)] = held
+            if j > i:
+                work_ref[pl.ds(j * width, width), pl.ds(i * width, width)] = jnp.zeros((width, width), jnp.float32)
+
+
+def factor_kernel(width, gram_ref, upper_ref, inverse_ref, work_ref):
     total = gram_ref.shape[0]
-    work_ref[...] = gram_ref[...]
+    if width is None:
+        work_ref[...] = gram_ref[...]
+    else:
+        unstack(gram_ref, work_ref, width)
     column = lax.broadcasted_iota(jnp.int32, (BLOCK, total), 1)
 
     @pl.loop(0, total // BLOCK)
@@ -96,35 +113,232 @@
             )
 
 
-def factor(gram):
+def factor(gram, width):
     total = gram.shape[0]
-    whole = jax.ShapeDtypeStruct(gram.shape, jnp.float32)
+    whole = jax.ShapeDtypeStruct((total, total), jnp.float32)
     return pl.pallas_call(
-        factor_kernel,
+        lambda *refs: factor_kernel(width, *refs),
         out_shape=(whole, whole),
         in_specs=[pl.BlockSpec(memory_space=pltpu.VMEM)],
         out_specs=(pl.BlockSpec(memory_space=pltpu.VMEM),) * 2,
-        scratch_shapes=[pltpu.VMEM(gram.shape, jnp.float32)],
+        scratch_shapes=[pltpu.VMEM((total, total), jnp.float32)],
         compiler_params=pltpu.CompilerParams(vmem_limit_bytes=32 * 1024 * 1024),
         cost_estimate=pl.CostEstimate(flops=60 * total**3, bytes_accessed=12 * total**2, transcendentals=0),
     )(gram)
 
 
-def local(panels_t, trailing_t):
+def remote(source, target, send, receive, row, col):
+    return pltpu.make_async_remote_copy(
+        src_ref=source,
+        dst_ref=target,
+        send_sem=send,
+        recv_sem=receive,
+        device_id=(row, col),
+        device_id_type=MESH,
+    )
+
+
+def greet(peers):
+    barrier = pltpu.get_barrier_semaphore()
+    for row, col in peers:
+        pl.semaphore_signal(barrier, inc=1, device_id=(row, col), device_id_type=MESH)
+    pl.semaphore_wait(barrier, len(peers))
+
+
+def column_peers(cols):
+    row, col = lax.axis_index("row"), lax.axis_index("col")
+    mate = col + 1 - 2 * lax.rem(col, 2)
+    return [(row, lax.rem(col + 2 * t, cols)) for t in range(1, cols // 2)] + [(row, mate)]
+
+
+def gather_columns(cols, pieces, ready, view, sems):
+    line_send, line_recv, mate_send, mate_recv = sems
+    row, col = lax.axis_index("row"), lax.axis_index("col")
+    mate = col + 1 - 2 * lax.rem(col, 2)
+    half = cols // 2
+    sent = []
+
+    def launch(copy):
+        copy.start()
+        sent.append(copy)
+
+    def to_mate(source, owner, s, t):
+        launch(remote(source, view(owner, s), mate_send.at[s, t], mate_recv.at[s, t], row, mate))
+
+    def relay(s):
+        for t in range(1, half):
+            owner = lax.rem(col - 2 * t + cols, cols)
+            place = view(owner, s)
+            remote(place, place, line_send.at[s, t], line_recv.at[s, t], row, mate).wait_recv()
+            to_mate(place, owner, s, t)
+
+    for s in range(pieces):
+        source = ready(s)
+        for t in range(1, half):
+            peer = lax.rem(col + 2 * t, cols)
+            launch(remote(source, view(col, s), line_send.at[s, t], line_recv.at[s, t], row, peer))
+        to_mate(source, col, s, 0)
+        if s > 0:
+            relay(s - 1)
+    relay(pieces - 1)
+    for s in range(pieces):
+        for t in range(half):
+            place = view(lax.rem(mate - 2 * t + cols, cols), s)
+            remote(place, place, mate_send.at[s, t], mate_recv.at[s, t], row, mate).wait_recv()
+    for copy in sent:
+        copy.wait_send()
+
+
+def panel_kernel(cols, pieces, block_ref, out_ref, *sems):
+    col = lax.axis_index("col")
+    greet(column_peers(cols))
+    rows = block_ref.shape[0] // pieces
+
+    def part(s):
+        return pl.ds(s * rows, rows)
+
+    gather_columns(cols, pieces, lambda s: block_ref.at[part(s)], lambda c, s: out_ref.at[c, part(s)], sems)
+    out_ref[col] = block_ref[...]
+
+
+def column_sems(cols, pieces):
+    return [pltpu.SemaphoreType.DMA((pieces, cols // 2))] * 4
+
+
+def gather_panel(block, cols):
+    pieces = 2
+    vmem = pl.BlockSpec(memory_space=pltpu.VMEM)
+    return pl.pallas_call(
+        lambda *refs: panel_kernel(cols, pieces, *refs),
+        out_shape=jax.ShapeDtypeStruct((cols,) + block.shape, jnp.float32),
+        in_specs=[vmem],
+        out_specs=vmem,
+        scratch_shapes=column_sems(cols, pieces),
+        compiler_params=pltpu.CompilerParams(collective_id=0, has_side_effects=True, vmem_limit_bytes=16 * 1024 * 1024),
+    )(block)
+
+
+def gram_kernel(rows, cols, part_ref, out_ref, land_ref, sum_send, sum_recv, row_send, row_recv, *sems):
+    row, col = lax.axis_index("row"), lax.axis_index("col")
+    peers = [(lax.rem(row + s, rows), col) for s in range(1, rows)]
+    greet(peers + column_peers(cols))
+    sent = []
+    for s in range(1, rows):
+        peer = lax.rem(row + s, rows)
+        copy = remote(part_ref.at[peer], land_ref.at[s], sum_send.at[s], sum_recv.at[s], peer, col)
+        copy.start()
+        sent.append(copy)
+    total = part_ref[row]
+    for s in range(1, rows):
+        sent[s - 1].wait_recv()
+        total = total + land_ref[s]
+    out_ref[col, row] = total
+
+    def view(c, s):
+        return out_ref.at[c, lax.rem(row - s + rows, rows)]
+
+    for s in range(1, rows):
+        peer = lax.rem(row + s, rows)
+        copy = remote(view(col, 0), view(col, 0), row_send.at[s], row_recv.at[s], peer, col)
+        copy.start()
+        sent.append(copy)
+
+    def ready(s):
+        if s > 0:
+            place = view(col, s)
+            remote(place, place, row_send.at[s], row_recv.at[s], lax.rem(row + s, rows), col).wait_recv()
+        return view(col, s)
+
+    gather_columns(cols, rows, ready, view, sems)
+    for copy in sent:
+        copy.wait_send()
+
+
+def gather_gram(part, cols):
+    rows = part.shape[0]
+    vmem = pl.BlockSpec(memory_space=pltpu.VMEM)
+    return pl.pallas_call(
+        lambda *refs: gram_kernel(rows, cols, *refs),
+        out_shape=jax.ShapeDtypeStruct((cols,) + part.shape, jnp.float32),
+        in_specs=[vmem],
+        out_specs=vmem,
+        scratch_shapes=[pltpu.VMEM(part.shape, jnp.float32)] + [pltpu.SemaphoreType.DMA((rows,))] * 4 + column_sems(cols, rows),
+        compiler_params=pltpu.CompilerParams(collective_id=1, has_side_effects=True, vmem_limit_bytes=24 * 1024 * 1024),
+        cost_estimate=pl.CostEstimate(flops=10**11, bytes_accessed=8 * cols * part.size, transcendentals=0),
+    )(part)
+
+
+def spread_kernel(rows, slab_ref, out_ref, send, receive):
+    row, col = lax.axis_index("row"), lax.axis_index("col")
+    greet([(lax.rem(row + s, rows), col) for s in range(1, rows)])
+    sent = []
+    for s in range(1, rows):
+        peer = lax.rem(row + s, rows)
+        copy = remote(slab_ref.at[peer], out_ref.at[row], send.at[s], receive.at[s], peer, col)
+        copy.start()
+        sent.append(copy)
+    out_ref[row] = slab_ref[row]
+    for s in range(1, rows):
+        place = out_ref.at[lax.rem(row - s + rows, rows)]
+        remote(place, place, send.at[s], receive.at[s], lax.rem(row + s, rows), col).wait_recv()
+    for copy in sent:
+        copy.wait_send()
+
+
+def spread_slab(slab):
+    rows = slab.shape[0]
+    vmem = pl.BlockSpec(memory_space=pltpu.VMEM)
+    return pl.pallas_call(
+        lambda *refs: spread_kernel(rows, *refs),
+        out_shape=jax.ShapeDtypeStruct(slab.shape, jnp.float32),
+        in_specs=[vmem],
+        out_specs=vmem,
+        scratch_shapes=[pltpu.SemaphoreType.DMA((rows,))] * 2,
+        compiler_params=pltpu.CompilerParams(collective_id=2, has_side_effects=True, vmem_limit_bytes=8 * 1024 * 1024),
+    )(slab)
+
+
+def direct(panels_t, trailing_t, rows, cols):
+    width, depth = panels_t.shape
+    total = width * cols
+    near = cols // 2 + 1
+    panel = gather_panel(panels_t, cols).reshape(total, depth)
+    turned = jnp.concatenate([panel, panel])
+    ring = lax.dynamic_slice_in_dim(turned, lax.axis_index("col") * width, near * width, 0)
+    part = product(panels_t, ring.T).reshape(rows, width // rows, near * width)
+    cross = lax.psum_scatter(product(trailing_t, panel.T), "row", scatter_dimension=0, tiled=True)
+    stacked = gather_gram(part, cols).reshape(total, near * width)
+    r_full, invert = factor(stacked, width)
+    slab = product(product(cross, invert.T), invert)
+    slab = slab.reshape(slab.shape[0], rows, total // rows).transpose(1, 0, 2)
+    spread = spread_slab(slab)
+    return r_full, spread.transpose(2, 0, 1).reshape(total // rows, -1)
+
+
+def plain(panels_t, trailing_t):
     panel = lax.all_gather(panels_t, "col", axis=0, tiled=True)
     gram_part = lax.psum_scatter(product(panels_t, panel.T), "row", scatter_dimension=0, tiled=True)
     gram = lax.all_gather(gram_part, ("col", "row"), axis=0, tiled=True)
     cross = lax.psum_scatter(product(trailing_t, panel.T), "row", scatter_dimension=0, tiled=True)
-    r_full, invert = factor(gram)
+    r_full, invert = factor(gram, None)
     slab = product(product(cross, invert.T), invert)
-    spread = lax.all_to_all(slab, "row", split_axis=1, concat_axis=0, tiled=True)
+    return r_full, lax.all_to_all(slab, "row", split_axis=1, concat_axis=0, tiled=True).T
+
+
+def local(panels_t, trailing_t):
+    rows, cols = lax.axis_size("row"), lax.axis_size("col")
+    width = panels_t.shape[0]
+    if width % BLOCK == 0 and width // rows % MICRO == 0 and cols % 2 == 0:
+        r_full, coef_block = direct(panels_t, trailing_t, rows, cols)
+    else:
+        r_full, coef_block = plain(panels_t, trailing_t)
     total = r_full.shape[0]
-    rows_out = total // lax.axis_size("row")
-    cols_out = total // lax.axis_size("col")
+    rows_out = total // rows
+    cols_out = total // cols
     row_start = lax.axis_index("row") * rows_out
     col_start = lax.axis_index("col") * cols_out
     r_block = lax.dynamic_slice(r_full, (row_start, col_start), (rows_out, cols_out))
-    return (r_block, spread.T)
+    return (r_block, coef_block)
 
 
 def solution(mesh):

time: 270 us -> 192 us (0.71)
  waiting for transfers between devices: 171 us -> 0.02 us
  Pallas kernels: 54.9 us -> 155 us
  starting transfers between devices: 3.83 us -> 0.04 us
    pallas_call x1 -> x4, Pallas kernels: 54.9 us -> 155 us  [the longest x1 68.3 us: gather_gram(): pl.pallas_call(lambda *refs: gram_kernel(rows, cols, *refs), out_shape=ja...]
    all_gather x2 -> x0, waiting for transfers between devices: 80.1 us -> none  [the longest x1 59.1 us: local(): gram = lax.all_gather(gram_part, ('col', 'row'), axis=0, tiled=True)]
    reduce_scatter x2 -> x1, waiting for transfers between devices: 80 us -> 0.01 us  [direct(): lax.psum_scatter(product(trailing_t, panel.T), 'row', scatter_dimension=0...]
    all_to_all x1 -> x0, waiting for transfers between devices: 9.88 us -> none  [local(): lax.all_to_all(slab, 'row', split_axis=1, concat_axis=0, tiled=True)]
    all_to_all x1 -> x0, starting transfers between devices: 3.68 us -> none  [local(): lax.all_to_all(slab, 'row', split_axis=1, concat_axis=0, tiled=True)]
    unnamed x13 -> x15, local copies, waits for them, and re-layouts: 7.03 us -> 7.44 us
  transfers between devices with their start and end apart: 5 -> 1, of which waited for: 5 -> 0; matrix products, arithmetic and copies ran while one was open for 2% -> 1% of each run, Pallas kernels for 20% -> 64%
where the time goes in v2:
time: 192 us
  Pallas kernels  155 us (81%)
  matrix products  14.5 us (8%)
  between operations  14.2 us (7%)
  local copies, waits for them, and re-layouts  8.13 us (4%)
    pallas_call x1, Pallas kernels, gather_gram(): pl.pallas_call(lambda *refs: gram_kernel(rows, cols, *refs), out_shape=ja...  68.3 us
    pallas_call x1, Pallas kernels, factor(): pl.pallas_call(lambda *refs: factor_kernel(width, *refs), out_shape=(whol...  54.9 us
    pallas_call x1, Pallas kernels, spread_slab(): pl.pallas_call(lambda *refs: spread_kernel(rows, *refs), out_shape=jax.Sh...  20.5 us
    dot_general x4, matrix products, product(): return jnp.dot(left, right, precision=lax.Precision.HIGHEST)  14.5 us
    pallas_call x1, Pallas kernels, gather_panel(): pl.pallas_call(lambda *refs: panel_kernel(cols, pieces, *refs), out_shape...  11.1 us
    unnamed x15, local copies, waits for them, and re-layouts  7.44 us
  transfers between devices with their start and end apart: 1, of which 0 were waited for; matrix products, arithmetic and copies ran while one was open for 1% of the time, Pallas kernels for 64%

profile of v2, /device:TPU:0, one launch (start us, length us, event | category | flops | bytes accessed | tf_op | source)
XLA Modules:
  0.0 191.7 jit_solution(10639625744758716226)
XLA Ops:
  7.2 0.0 copy-start
  7.2 0.0 reduce-scatter.2.cloned.1.call-start
  7.2 0.0 copy-start.3
  7.2 1.0 copy-done.3
  8.2 11.1 %shard_map.41 = f32[4,256,256]{2,1,0:T(8,128)S(1)} custom-call(f32[256,256]{1,0:T(8,128)S(1)} %copy-done.3), custom_call_target="tpu_custom_call" | custom-call | tf_op jit(solution)/shard_map/pallas_call | solution.py:211
  19.4 0.0 copy-start.4
  19.4 0.0 copy-done
  19.4 4.4 %fusion.5 = f32[768,1024]{1,0:T(8,128)} fusion(f32[768,256]{1,0:T(8,128)S(1)} %copy-done, f32[1024,256]{1,0:T(8,128)S(1)} %bitcast.23), kind=kOutput, calls=%fused_computation.8 | convolution fusion | flops 2415919104 | bytes 4980736 | tf_op jit(solution)/shard_map/dot_general | solution.py:14
  23.8 0.0 reduce-scatter.2.cloned.1.call-update
  23.8 0.0 copy-done.4
  23.8 1.0 fusion.1
  24.8 68.3 %shard_map.42 = f32[4,8,32,768]{3,2,1,0:T(8,128)S(1)} custom-call(f32[8,32,768]{2,1,0:T(8,128)S(1)} %bitcast.27), custom_call_target="tpu_custom_call" | custom-call | flops 99999997952 | bytes 6291456 | tf_op jit(solution)/shard_map/pallas_call | solution.py:260
  93.1 0.0 copy-start.5
  93.1 1.6 copy-done.5
  94.7 1.9 %copy-done.6 = f32[4,8,32,768]{3,2,1,0:T(8,128)S(1)} copy-done((f32[4,8,32,768]{3,2,1,0:T(8,128)S(1)}, f32[4,8,32,768]{3,2,1,0:T(8,128)}, u32[]{:S(2)}) %copy-start.6) | copy-done | bytes 3145752
  96.7 54.9 %shard_map.43 = (f32[1024,1024]{1,0:T(8,128)S(1)}, f32[1024,1024]{1,0:T(8,128)S(1)}) custom-call(f32[1024,768]{1,0:T(8,128)S(1)} %bitcast.28), custom_call_target="tpu_custom_call" | custom-call | flops 64424509440 | bytes 12582912 | tf_op jit(solution)/shard_map/pallas_call | solution.py:119
  151.6 0.0 copy-start.1
  151.6 1.9 %copy-done.1 = f32[1024,1024]{1,0:T(8,128)} copy-done((f32[1024,1024]{1,0:T(8,128)}, f32[1024,1024]{1,0:T(8,128)S(1)}, u32[]{:S(2)}) %copy-start.1) | copy-done | bytes 4194328
  153.5 0.7 dynamic_slice.7
  154.2 6.6 %fusion.6 = f32[96,1024]{1,0:T(8,128)S(1)} fusion(f32[96,1024]{1,0:T(8,128)} %reduce-scatter.2.cloned.1.call-done, f32[1024,1024]{1,0:T(8,128)} %copy-done.1), kind=kOutput, calls=%fused_computation.9 | convolution fusion | flops 1207959552 | bytes 4980736 | tf_op jit(solution)/shard_map/dot_general | solution.py:14
  160.8 0.0 copy-done.2
  160.8 2.6 %convolution_bitcast_fusion = f32[12,8,8,128]{3,2,1,0:T(8,128)S(1)} fusion(f32[96,1024]{1,0:T(8,128)S(1)} %fusion.6, f32[1024,1024]{1,0:T(8,128)S(1)} %copy-done.2), kind=kOutput, calls=%fused_computation.2 | convolution fusion | flops 1207959552 | bytes 4980736 | tf_op jit(solution)/shard_map/dot_general | solution.py:14
  163.4 20.5 %shard_map.44 = f32[8,96,128]{2,1,0:T(8,128)S(1)} custom-call(f32[8,96,128]{2,1,0:T(8,128)S(1)} %bitcast.25), custom_call_target="tpu_custom_call" | custom-call | tf_op jit(solution)/shard_map/pallas_call | solution.py:291
  183.9 0.9 copy.6
  (4 shorter events, 0.0 us)
Async XLA Ops:
  7.2 12.2 %copy-start = (f32[768,256]{1,0:T(8,128)S(1)}, f32[768,256]{1,0:T(8,128)}, u32[]{:S(2)}) copy-start(f32[768,256]{1,0:T(8,128)} %param.3) | copy-start | bytes 2359300
  7.2 147.0 %reduce-scatter.2.cloned.1.call-start = ((), (), s32[]{:S(2)}) async-start(), calls=%async_computation.1 | async-start | bytes 3538944 | tf_op jit(solution)/shard_map/reduce_scatter | solution.py:309
  7.2 1.0 copy-start.3
  19.4 4.4 %copy-start.4 = (f32[256,256]{1,0:T(8,128)S(1)}, f32[256,256]{1,0:T(8,128)}, u32[]{:S(2)}) copy-start(f32[256,256]{1,0:T(8,128)} %refs_0_.1) | copy-start | bytes 786436
  93.1 1.6 copy-start.5
  94.7 1.9 %copy-start.6 = (f32[4,8,32,768]{3,2,1,0:T(8,128)S(1)}, f32[4,8,32,768]{3,2,1,0:T(8,128)}, u32[]{:S(2)}) copy-start(f32[4,8,32,768]{3,2,1,0:T(8,128)} %copy-done.5) | copy-start | bytes 9437188
  151.6 1.9 %copy-start.1 = (f32[1024,1024]{1,0:T(8,128)}, f32[1024,1024]{1,0:T(8,128)S(1)}, u32[]{:S(2)}) copy-start(f32[1024,1024]{1,0:T(8,128)S(1)} %get-tuple-element.5) | copy-start | bytes 12582916
  154.2 6.6 %copy-start.2 = (f32[1024,1024]{1,0:T(8,128)S(1)}, f32[1024,1024]{1,0:T(8,128)}, u32[]{:S(2)}) copy-start(f32[1024,1024]{1,0:T(8,128)} %copy-done.1) | copy-start | bytes 12582916
Sparse Core Ops, SparseCore 0:
  23.9 102.7 reduce-scatter.1

commit v3 on v2

--- a/solution.py
+++ b/solution.py
@@ -12,6 +12,16 @@
 
 def product(left, right):
     return jnp.dot(left, right, precision=lax.Precision.HIGHEST)
+
+
+def contract(left, right, left_dim, right_dim):
+    return lax.dot_general(
+        left,
+        right,
+        (((left_dim,), (right_dim,)), ((), ())),
+        precision=lax.Precision.HIGHEST,
+        preferred_element_type=jnp.float32,
+    )
 
 
 def lanes(tile, lane):
@@ -67,28 +77,26 @@
 
 
 def unstack(stacked_ref, work_ref, width):
-    count = stacked_ref.shape[0] // width
+    count = stacked_ref.shape[0]
+
+    def block(i, step):
+        return stacked_ref[i, :, :, pl.ds(step * width, width)].reshape(width, width)
+
     for i in range(count):
         for j in range(i, count):
-            if j - i <= count // 2:
-                held = stacked_ref[pl.ds(i * width, width), pl.ds((j - i) * width, width)]
-            else:
-                held = stacked_ref[pl.ds(j * width, width), pl.ds((count + i - j) * width, width)].T
+            held = block(i, j - i) if j - i <= count // 2 else block(j, count + i - j).T
             work_ref[pl.ds(i * width, width), pl.ds(j * width, width)] = held
             if j > i:
                 work_ref[pl.ds(j * width, width), pl.ds(i * width, width)] = jnp.zeros((width, width), jnp.float32)
 
 
-def factor_kernel(width, gram_ref, upper_ref, inverse_ref, work_ref):
-    total = gram_ref.shape[0]
-    if width is None:
-        work_ref[...] = gram_ref[...]
-    else:
-        unstack(gram_ref, work_ref, width)
+def factor_loop(upper_ref, inverse_ref, work_ref, beside):
+    total = work_ref.shape[0]
     column = lax.broadcasted_iota(jnp.int32, (BLOCK, total), 1)
 
     @pl.loop(0, total // BLOCK)
     def _(k):
+        beside(k)
         start = pl.multiple_of(k * BLOCK, BLOCK)
         here = pl.ds(start, BLOCK)
         diagonal, inverse = factor_block(work_ref[here, here])
@@ -104,20 +112,19 @@
         def _(i):
             there = pl.ds(pl.multiple_of(i * BLOCK, BLOCK), BLOCK)
             work_ref[there, here] = jnp.zeros((BLOCK, BLOCK), jnp.float32)
-            work_ref[there, :] -= lax.dot_general(
-                work_ref[here, there],
-                work_ref[here, :],
-                (((0,), (0,)), ((), ())),
-                precision=lax.Precision.HIGHEST,
-                preferred_element_type=jnp.float32,
-            )
-
-
-def factor(gram, width):
+            work_ref[there, :] -= contract(work_ref[here, there], work_ref[here, :], 0, 0)
+
+
+def factor_kernel(gram_ref, upper_ref, inverse_ref, work_ref):
+    work_ref[...] = gram_ref[...]
+    factor_loop(upper_ref, inverse_ref, work_ref, lambda k: None)
+
+
+def factor(gram):
     total = gram.shape[0]
     whole = jax.ShapeDtypeStruct((total, total), jnp.float32)
     return pl.pallas_call(
-        lambda *refs: factor_kernel(width, *refs),
+        factor_kernel,
         out_shape=(whole, whole),
         in_specs=[pl.BlockSpec(memory_space=pltpu.VMEM)],
         out_specs=(pl.BlockSpec(memory_space=pltpu.VMEM),) * 2,
@@ -218,16 +225,17 @@
     )(block)
 
 
-def gram_kernel(rows, cols, part_ref, out_ref, land_ref, sum_send, sum_recv, row_send, row_recv, *sems):
+def reduce_gram(rows, cols, part_ref, out_ref, land_ref, sums, gathers, column, between):
     row, col = lax.axis_index("row"), lax.axis_index("col")
-    peers = [(lax.rem(row + s, rows), col) for s in range(1, rows)]
-    greet(peers + column_peers(cols))
+    sum_send, sum_recv = sums
+    row_send, row_recv = gathers
     sent = []
     for s in range(1, rows):
         peer = lax.rem(row + s, rows)
         copy = remote(part_ref.at[peer], land_ref.at[s], sum_send.at[s], sum_recv.at[s], peer, col)
         copy.start()
         sent.append(copy)
+    between()
     total = part_ref[row]
     for s in range(1, rows):
         sent[s - 1].wait_recv()
@@ -249,28 +257,26 @@
             remote(place, place, row_send.at[s], row_recv.at[s], lax.rem(row + s, rows), col).wait_recv()
         return view(col, s)
 
-    gather_columns(cols, rows, ready, view, sems)
+    gather_columns(cols, rows, ready, view, column)
     for copy in sent:
         copy.wait_send()
 
 
-def gather_gram(part, cols):
-    rows = part.shape[0]
-    vmem = pl.BlockSpec(memory_space=pltpu.VMEM)
-    return pl.pallas_call(
-        lambda *refs: gram_kernel(rows, cols, *refs),
-        out_shape=jax.ShapeDtypeStruct((cols,) + part.shape, jnp.float32),
-        in_specs=[vmem],
-        out_specs=vmem,
-        scratch_shapes=[pltpu.VMEM(part.shape, jnp.float32)] + [pltpu.SemaphoreType.DMA((rows,))] * 4 + column_sems(cols, rows),
-        compiler_params=pltpu.CompilerParams(collective_id=1, has_side_effects=True, vmem_limit_bytes=24 * 1024 * 1024),
-        cost_estimate=pl.CostEstimate(flops=10**11, bytes_accessed=8 * cols * part.size, transcendentals=0),
-    )(part)
-
-
-def spread_kernel(rows, slab_ref, out_ref, send, receive):
+def solve(cross_ref, row, inverse_ref, middle_ref, slab_ref):
+    total = inverse_ref.shape[0]
+    step = 2 * BLOCK
+    for j in range(0, total, step):
+        stop = j + step
+        middle_ref[:, j:stop] = contract(cross_ref[row, :, :stop], inverse_ref[j:stop, :stop], 1, 1)
+    wide = total // slab_ref.shape[0]
+    for j in range(0, total, step):
+        found = contract(middle_ref[:, j:], inverse_ref[j:, j : j + step], 1, 0)
+        for t in range(0, step, wide):
+            slab_ref[(j + t) // wide] = found[:, t : t + wide]
+
+
+def spread_slab(rows, slab_ref, out_ref, send, receive):
     row, col = lax.axis_index("row"), lax.axis_index("col")
-    greet([(lax.rem(row + s, rows), col) for s in range(1, rows)])
     sent = []
     for s in range(1, rows):
         peer = lax.rem(row + s, rows)
@@ -285,17 +291,63 @@
         copy.wait_send()
 
 
-def spread_slab(slab):
-    rows = slab.shape[0]
-    vmem = pl.BlockSpec(memory_space=pltpu.VMEM)
-    return pl.pallas_call(
-        lambda *refs: spread_kernel(rows, *refs),
-        out_shape=jax.ShapeDtypeStruct(slab.shape, jnp.float32),
-        in_specs=[vmem],
-        out_specs=vmem,
-        scratch_shapes=[pltpu.SemaphoreType.DMA((rows,))] * 2,
-        compiler_params=pltpu.CompilerParams(collective_id=2, has_side_effects=True, vmem_limit_bytes=8 * 1024 * 1024),
-    )(slab)
+def main_kernel(rows, cols, width, *refs):
+    part_ref, trailing_ref, panel_ref, upper_out, coef_out = refs[:5]
+    stacked_ref, land_ref, cross_ref, pair_ref, line_ref, work_ref, upper_ref, inverse_ref, middle_ref, slab_ref = refs[5:15]
+    sums, gathers, spreads, pairs, lines = (refs[15 + 2 * i : 17 + 2 * i] for i in range(5))
+    column = refs[25:]
+    row, col = lax.axis_index("row"), lax.axis_index("col")
+    half = rows // 2
+    place, side = row // 2, lax.rem(row, 2)
+    greet([(lax.rem(row + s, rows), col) for s in range(1, rows)] + column_peers(cols))
+
+    def multiply():
+        @pl.loop(0, rows)
+        def _(r):
+            cross_ref[r] = contract(trailing_ref[r], panel_ref[...], 1, 1)
+
+    reduce_gram(rows, cols, part_ref, stacked_ref, land_ref, sums, gathers, column, multiply)
+
+    def target(s, which):
+        return 2 * lax.rem(place + s, half) + which
+
+    def pair_copy(s):
+        mate = 2 * place + 1 - side
+        return remote(cross_ref.at[target(s, 1 - side)], pair_ref.at[s], pairs[0].at[s], pairs[1].at[s], mate, col)
+
+    def line_copy(s):
+        owner = target(s, side)
+        return remote(cross_ref.at[owner], line_ref.at[s], lines[0].at[s], lines[1].at[s], owner, col)
+
+    def fold(s):
+        pair_copy(s).wait_recv()
+        cross_ref[target(s, side)] += pair_ref[s]
+        if s > 0:
+            line_copy(s).start()
+
+    for s in list(range(1, half)) + [0]:
+        pair_copy(s).start()
+    unstack(stacked_ref, work_ref, width)
+
+    def beside(k):
+        for s in range(1, half):
+            pl.when(k == s + 1)(lambda s=s: fold(s))
+
+    factor_loop(upper_ref, inverse_ref, work_ref, beside)
+    upper_out[...] = upper_ref[
+        pl.ds(pl.multiple_of(row * upper_out.shape[0], MICRO), upper_out.shape[0]),
+        pl.ds(pl.multiple_of(col * upper_out.shape[1], BLOCK), upper_out.shape[1]),
+    ]
+    fold(0)
+    for s in range(1, half):
+        line_copy(s).wait_recv()
+        cross_ref[row] += line_ref[s]
+    solve(cross_ref, row, inverse_ref, middle_ref, slab_ref)
+    spread_slab(rows, slab_ref, coef_out, *spreads)
+    for s in range(half):
+        pair_copy(s).wait_send()
+        if s > 0:
+            line_copy(s).wait_send()
 
 
 def direct(panels_t, trailing_t, rows, cols):
@@ -306,13 +358,34 @@
     turned = jnp.concatenate([panel, panel])
     ring = lax.dynamic_slice_in_dim(turned, lax.axis_index("col") * width, near * width, 0)
     part = product(panels_t, ring.T).reshape(rows, width // rows, near * width)
-    cross = lax.psum_scatter(product(trailing_t, panel.T), "row", scatter_dimension=0, tiled=True)
-    stacked = gather_gram(part, cols).reshape(total, near * width)
-    r_full, invert = factor(stacked, width)
-    slab = product(product(cross, invert.T), invert)
-    slab = slab.reshape(slab.shape[0], rows, total // rows).transpose(1, 0, 2)
-    spread = spread_slab(slab)
-    return r_full, spread.transpose(2, 0, 1).reshape(total // rows, -1)
+    trailing = trailing_t.reshape(rows, -1, depth)
+    thick = trailing.shape[1]
+    vmem = pl.BlockSpec(memory_space=pltpu.VMEM)
+    shapes = [
+        (cols,) + part.shape,
+        part.shape,
+        (rows, thick, total),
+        (rows // 2, thick, total),
+        (rows // 2, thick, total),
+        (total, total),
+        (total, total),
+        (total, total),
+        (thick, total),
+        (rows, thick, total // rows),
+    ]
+    semaphores = [pltpu.SemaphoreType.DMA((rows,))] * 6 + [pltpu.SemaphoreType.DMA((rows // 2,))] * 4
+    r_block, spread = pl.pallas_call(
+        lambda *refs: main_kernel(rows, cols, width, *refs),
+        out_shape=(
+            jax.ShapeDtypeStruct((total // rows, total // cols), jnp.float32),
+            jax.ShapeDtypeStruct((rows, thick, total // rows), jnp.float32),
+        ),
+        in_specs=[vmem] * 3,
+        out_specs=(vmem, vmem),
+        scratch_shapes=[pltpu.VMEM(shape, jnp.float32) for shape in shapes] + semaphores + column_sems(cols, rows),
+        compiler_params=pltpu.CompilerParams(collective_id=1, has_side_effects=True, vmem_limit_bytes=48 * 1024 * 1024),
+    )(part, trailing, panel)
+    return r_block, spread.transpose(2, 0, 1).reshape(total // rows, -1)
 
 
 def plain(panels_t, trailing_t):
@@ -320,7 +393,7 @@
     gram_part = lax.psum_scatter(product(panels_t, panel.T), "row", scatter_dimension=0, tiled=True)
     gram = lax.all_gather(gram_part, ("col", "row"), axis=0, tiled=True)
     cross = lax.psum_scatter(product(trailing_t, panel.T), "row", scatter_dimension=0, tiled=True)
-    r_full, invert = factor(gram, None)
+    r_full, invert = factor(gram)
     slab = product(product(cross, invert.T), invert)
     return r_full, lax.all_to_all(slab, "row", split_axis=1, concat_axis=0, tiled=True).T
 
@@ -328,16 +401,16 @@
 def local(panels_t, trailing_t):
     rows, cols = lax.axis_size("row"), lax.axis_size("col")
     width = panels_t.shape[0]
-    if width % BLOCK == 0 and width // rows % MICRO == 0 and cols % 2 == 0:
-        r_full, coef_block = direct(panels_t, trailing_t, rows, cols)
-    else:
-        r_full, coef_block = plain(panels_t, trailing_t)
-    total = r_full.shape[0]
+    total = width * cols
+    thick = trailing_t.shape[0] // rows
+    tiled = width % BLOCK == 0 and total // rows % BLOCK == 0 and width // rows % MICRO == 0 and thick % MICRO == 0
+    if tiled and rows % 2 == 0 and cols % 2 == 0 and rows // 2 < total // BLOCK:
+        return direct(panels_t, trailing_t, rows, cols)
+    r_full, coef_block = plain(panels_t, trailing_t)
     rows_out = total // rows
-    cols_out = total // cols
     row_start = lax.axis_index("row") * rows_out
-    col_start = lax.axis_index("col") * cols_out
-    r_block = lax.dynamic_slice(r_full, (row_start, col_start), (rows_out, cols_out))
+    col_start = lax.axis_index("col") * width
+    r_block = lax.dynamic_slice(r_full, (row_start, col_start), (rows_out, width))
     return (r_block, coef_block)
 
 

time: 192 us -> 140 us (0.73)
  Pallas kernels: 155 us -> 135 us
  between operations: 14.2 us -> 0.67 us
  matrix products: 14.5 us -> 0.99 us
  local copies, waits for them, and re-layouts: 8.13 us -> 2.65 us
    pallas_call x3 -> x1, Pallas kernels: 144 us -> 124 us  [direct(): pl.pallas_call(lambda *refs: main_kernel(rows, cols, width, *refs), out_s...]
    dot_general x4 -> x1, matrix products: 14.5 us -> 0.99 us  [product(): return jnp.dot(left, right, precision=lax.Precision.HIGHEST)]
    unnamed x15 -> x6, local copies, waits for them, and re-layouts: 7.44 us -> 2.65 us
  transfers between devices with their start and end apart: 1 -> 0, of which waited for: 0 -> 0; matrix products, arithmetic and copies ran while one was open for 1% -> 0% of each run, Pallas kernels for 64% -> 0%
where the time goes in v3:
time: 140 us; the launch traced here: 139 us
  Pallas kernels  135 us (96%)
  local copies, waits for them, and re-layouts  2.65 us (2%)
    pallas_call x1, Pallas kernels, direct(): pl.pallas_call(lambda *refs: main_kernel(rows, cols, width, *refs), out_s...  124 us
    pallas_call x1, Pallas kernels, gather_panel(): pl.pallas_call(lambda *refs: panel_kernel(cols, pieces, *refs), out_shape...  11.1 us

profile of v3, /device:TPU:0, one launch (start us, length us, event | category | flops | bytes accessed | tf_op | source)
XLA Modules:
  0.0 139.4 jit_solution(15164373082909923704)
XLA Ops:
  0.6 0.0 copy-start
  0.6 0.9 copy-done
  1.6 11.1 %shard_map.41 = f32[4,256,256]{2,1,0:T(8,128)S(1)} custom-call(f32[256,256]{1,0:T(8,128)S(1)} %copy-done), custom_call_target="tpu_custom_call" | custom-call | tf_op jit(solution)/shard_map/pallas_call | solution.py:218
  12.7 0.0 copy-start.1
  12.7 1.0 fusion.1
  13.7 0.1 copy-done.1
  13.8 124.0 %shard_map.42 = (f32[128,256]{1,0:T(8,128)S(1)}, f32[8,96,128]{2,1,0:T(8,128)S(1)}) custom-call(f32[8,32,768]{2,1,0:T(8,128)S(1)} %bitcast.11, f32[8,96,256]{2,1,0:T(8,128)S(1)} %bitcast.12, f32[1024,256]{1,0:T(8,128)S(1)} %bitcast.10), custom_call_target="tpu_custom_call" | custom-call | tf_op jit(solution)/shard_map/pallas_call | solution.py:377
  137.8 0.9 copy.4
  138.7 0.7 copy.6
Async XLA Ops:
  0.6 1.0 copy-start
  12.7 1.1 copy-start.1

commit v4 on v3

--- a/solution.py
+++ b/solution.py
@@ -196,50 +196,76 @@
         copy.wait_send()
 
 
-def panel_kernel(cols, pieces, block_ref, out_ref, *sems):
-    col = lax.axis_index("col")
-    greet(column_peers(cols))
-    rows = block_ref.shape[0] // pieces
-
-    def part(s):
-        return pl.ds(s * rows, rows)
-
-    gather_columns(cols, pieces, lambda s: block_ref.at[part(s)], lambda c, s: out_ref.at[c, part(s)], sems)
-    out_ref[col] = block_ref[...]
-
-
 def column_sems(cols, pieces):
     return [pltpu.SemaphoreType.DMA((pieces, cols // 2))] * 4
 
 
-def gather_panel(block, cols):
-    pieces = 2
-    vmem = pl.BlockSpec(memory_space=pltpu.VMEM)
-    return pl.pallas_call(
-        lambda *refs: panel_kernel(cols, pieces, *refs),
-        out_shape=jax.ShapeDtypeStruct((cols,) + block.shape, jnp.float32),
-        in_specs=[vmem],
-        out_specs=vmem,
-        scratch_shapes=column_sems(cols, pieces),
-        compiler_params=pltpu.CompilerParams(collective_id=0, has_side_effects=True, vmem_limit_bytes=16 * 1024 * 1024),
-    )(block)
-
-
-def reduce_gram(rows, cols, part_ref, out_ref, land_ref, sums, gathers, column, between):
+def gather_panel(cols, block_ref, panel_ref, sems):
+    pieces = sems[0].shape[0]
+    size = block_ref.shape[0] // pieces
+
+    def part(s):
+        return pl.ds(s * size, size)
+
+    gather_columns(cols, pieces, lambda s: block_ref.at[part(s)], lambda c, s: panel_ref.at[c, part(s)], sems)
+    panel_ref[lax.axis_index("col")] = block_ref[...]
+
+
+class Reduction:
+    def __init__(self, rows, buffer_ref, pair_ref, line_ref, pairs, lines):
+        self.buffer, self.pair, self.line = buffer_ref, pair_ref, line_ref
+        self.pairs, self.lines = pairs, lines
+        self.row, self.col = lax.axis_index("row"), lax.axis_index("col")
+        self.half = rows // 2
+        self.place, self.side = self.row // 2, lax.rem(self.row, 2)
+
+    def target(self, s, which):
+        return 2 * lax.rem(self.place + s, self.half) + which
+
+    def pair_copy(self, s):
+        mate = 2 * self.place + 1 - self.side
+        source = self.buffer.at[self.target(s, 1 - self.side)]
+        return remote(source, self.pair.at[s], self.pairs[0].at[s], self.pairs[1].at[s], mate, self.col)
+
+    def line_copy(self, s):
+        owner = self.target(s, self.side)
+        source = self.buffer.at[owner]
+        return remote(source, self.line.at[s], self.lines[0].at[s], self.lines[1].at[s], owner, self.col)
+
+    def start(self):
+        for s in list(range(1, self.half)) + [0]:
+            self.pair_copy(s).start()
+
+    def fold(self, s):
+        self.pair_copy(s).wait_recv()
+        self.buffer[self.target(s, self.side)] += self.pair[s]
+        if s > 0:
+            self.line_copy(s).start()
+
+    def finish(self):
+        self.fold(0)
+        total = self.buffer[self.row]
+        for s in range(1, self.half):
+            self.line_copy(s).wait_recv()
+            total = total + self.line[s]
+        return total
+
+    def drain(self):
+        for s in range(self.half):
+            self.pair_copy(s).wait_send()
+            if s > 0:
+                self.line_copy(s).wait_send()
+
+
+def reduce_gram(rows, cols, reduction, out_ref, gathers, column, between):
     row, col = lax.axis_index("row"), lax.axis_index("col")
-    sum_send, sum_recv = sums
     row_send, row_recv = gathers
+    reduction.start()
+    for s in range(1, rows // 2):
+        reduction.fold(s)
+    between()
     sent = []
-    for s in range(1, rows):
-        peer = lax.rem(row + s, rows)
-        copy = remote(part_ref.at[peer], land_ref.at[s], sum_send.at[s], sum_recv.at[s], peer, col)
-        copy.start()
-        sent.append(copy)
-    between()
-    total = part_ref[row]
-    for s in range(1, rows):
-        sent[s - 1].wait_recv()
-        total = total + land_ref[s]
+    total = reduction.finish()
     out_ref[col, row] = total
 
     def view(c, s):
@@ -260,14 +286,15 @@
     gather_columns(cols, rows, ready, view, column)
     for copy in sent:
         copy.wait_send()
-
-
-def solve(cross_ref, row, inverse_ref, middle_ref, slab_ref):
+    reduction.drain()
+
+
+def solve(cross_ref, inverse_ref, middle_ref, slab_ref):
     total = inverse_ref.shape[0]
     step = 2 * BLOCK
     for j in range(0, total, step):
         stop = j + step
-        middle_ref[:, j:stop] = contract(cross_ref[row, :, :stop], inverse_ref[j:stop, :stop], 1, 1)
+        middle_ref[:, j:stop] = contract(cross_ref[:, :stop], inverse_ref[j:stop, :stop], 1, 1)
     wide = total // slab_ref.shape[0]
     for j in range(0, total, step):
         found = contract(middle_ref[:, j:], inverse_ref[j:, j : j + step], 1, 0)
@@ -292,99 +319,85 @@
 
 
 def main_kernel(rows, cols, width, *refs):
-    part_ref, trailing_ref, panel_ref, upper_out, coef_out = refs[:5]
-    stacked_ref, land_ref, cross_ref, pair_ref, line_ref, work_ref, upper_ref, inverse_ref, middle_ref, slab_ref = refs[5:15]
-    sums, gathers, spreads, pairs, lines = (refs[15 + 2 * i : 17 + 2 * i] for i in range(5))
-    column = refs[25:]
+    block_ref, trailing_ref, upper_out, coef_out = refs[:4]
+    panel_ref, part_ref, near_pair_ref, near_line_ref, stacked_ref = refs[4:9]
+    cross_ref, pair_ref, line_ref, work_ref, upper_ref, inverse_ref, summed_ref, middle_ref, slab_ref = refs[9:18]
+    gathers, spreads, near_pairs, near_lines, pairs, lines = (refs[18 + 2 * i : 20 + 2 * i] for i in range(6))
+    first, column = refs[30:34], refs[34:38]
     row, col = lax.axis_index("row"), lax.axis_index("col")
-    half = rows // 2
-    place, side = row // 2, lax.rem(row, 2)
     greet([(lax.rem(row + s, rows), col) for s in range(1, rows)] + column_peers(cols))
+    gather_panel(cols, block_ref, panel_ref, first)
+    for step in range(cols // 2 + 1):
+        held = contract(block_ref[...], panel_ref[lax.rem(col + step, cols)], 1, 1)
+        part_ref[:, :, step * width : (step + 1) * width] = held.reshape(rows, width // rows, width)
 
     def multiply():
+        panel = panel_ref[...].reshape(width * cols, panel_ref.shape[2])
+
         @pl.loop(0, rows)
         def _(r):
-            cross_ref[r] = contract(trailing_ref[r], panel_ref[...], 1, 1)
-
-    reduce_gram(rows, cols, part_ref, stacked_ref, land_ref, sums, gathers, column, multiply)
-
-    def target(s, which):
-        return 2 * lax.rem(place + s, half) + which
-
-    def pair_copy(s):
-        mate = 2 * place + 1 - side
-        return remote(cross_ref.at[target(s, 1 - side)], pair_ref.at[s], pairs[0].at[s], pairs[1].at[s], mate, col)
-
-    def line_copy(s):
-        owner = target(s, side)
-        return remote(cross_ref.at[owner], line_ref.at[s], lines[0].at[s], lines[1].at[s], owner, col)
-
-    def fold(s):
-        pair_copy(s).wait_recv()
-        cross_ref[target(s, side)] += pair_ref[s]
-        if s > 0:
-            line_copy(s).start()
-
-    for s in list(range(1, half)) + [0]:
-        pair_copy(s).start()
+            cross_ref[r] = contract(trailing_ref[r], panel, 1, 1)
+
+    near = Reduction(rows, part_ref, near_pair_ref, near_line_ref, near_pairs, near_lines)
+    reduce_gram(rows, cols, near, stacked_ref, gathers, column, multiply)
+    wide = Reduction(rows, cross_ref, pair_ref, line_ref, pairs, lines)
+    wide.start()
     unstack(stacked_ref, work_ref, width)
 
     def beside(k):
-        for s in range(1, half):
-            pl.when(k == s + 1)(lambda s=s: fold(s))
+        for s in range(1, rows // 2):
+            pl.when(k == s + 1)(lambda s=s: wide.fold(s))
 
     factor_loop(upper_ref, inverse_ref, work_ref, beside)
     upper_out[...] = upper_ref[
         pl.ds(pl.multiple_of(row * upper_out.shape[0], MICRO), upper_out.shape[0]),
         pl.ds(pl.multiple_of(col * upper_out.shape[1], BLOCK), upper_out.shape[1]),
     ]
-    fold(0)
-    for s in range(1, half):
-        line_copy(s).wait_recv()
-        cross_ref[row] += line_ref[s]
-    solve(cross_ref, row, inverse_ref, middle_ref, slab_ref)
+    summed_ref[...] = wide.finish()
+    solve(summed_ref, inverse_ref, middle_ref, slab_ref)
     spread_slab(rows, slab_ref, coef_out, *spreads)
-    for s in range(half):
-        pair_copy(s).wait_send()
-        if s > 0:
-            line_copy(s).wait_send()
+    wide.drain()
 
 
 def direct(panels_t, trailing_t, rows, cols):
     width, depth = panels_t.shape
     total = width * cols
-    near = cols // 2 + 1
-    panel = gather_panel(panels_t, cols).reshape(total, depth)
-    turned = jnp.concatenate([panel, panel])
-    ring = lax.dynamic_slice_in_dim(turned, lax.axis_index("col") * width, near * width, 0)
-    part = product(panels_t, ring.T).reshape(rows, width // rows, near * width)
+    half = rows // 2
     trailing = trailing_t.reshape(rows, -1, depth)
     thick = trailing.shape[1]
+    near = (width // rows, (cols // 2 + 1) * width)
     vmem = pl.BlockSpec(memory_space=pltpu.VMEM)
     shapes = [
-        (cols,) + part.shape,
-        part.shape,
+        (cols, width, depth),
+        (rows,) + near,
+        (half,) + near,
+        (half,) + near,
+        (cols, rows) + near,
         (rows, thick, total),
-        (rows // 2, thick, total),
-        (rows // 2, thick, total),
+        (half, thick, total),
+        (half, thick, total),
         (total, total),
         (total, total),
         (total, total),
         (thick, total),
+        (thick, total),
         (rows, thick, total // rows),
     ]
-    semaphores = [pltpu.SemaphoreType.DMA((rows,))] * 6 + [pltpu.SemaphoreType.DMA((rows // 2,))] * 4
+    semaphores = [pltpu.SemaphoreType.DMA((rows,))] * 4 + [pltpu.SemaphoreType.DMA((half,))] * 8
     r_block, spread = pl.pallas_call(
         lambda *refs: main_kernel(rows, cols, width, *refs),
         out_shape=(
             jax.ShapeDtypeStruct((total // rows, total // cols), jnp.float32),
             jax.ShapeDtypeStruct((rows, thick, total // rows), jnp.float32),
         ),
-        in_specs=[vmem] * 3,
+        in_specs=[vmem] * 2,
         out_specs=(vmem, vmem),
-        scratch_shapes=[pltpu.VMEM(shape, jnp.float32) for shape in shapes] + semaphores + column_sems(cols, rows),
+        scratch_shapes=[pltpu.VMEM(shape, jnp.float32) for shape in shapes]
+        + semaphores
+        + column_sems(cols, 2)
+        + column_sems(cols, rows),
         compiler_params=pltpu.CompilerParams(collective_id=1, has_side_effects=True, vmem_limit_bytes=48 * 1024 * 1024),
-    )(part, trailing, panel)
+    )(panels_t, trailing)
     return r_block, spread.transpose(2, 0, 1).reshape(total // rows, -1)
 
 

time: 140 us -> 134 us (0.957)
  Pallas kernels: 135 us -> 129 us
    pallas_call x1 -> x0, Pallas kernels: 11.1 us -> none  [gather_panel(): pl.pallas_call(lambda *refs: panel_kernel(cols, pieces, *refs), out_shape...]
    pallas_call x1, Pallas kernels: 124 us -> 129 us  [direct(): pl.pallas_call(lambda *refs: main_kernel(rows, cols, width, *refs), out_s...]
where the time goes in v4:
time: 134 us
  Pallas kernels  129 us (96%)
  local copies, waits for them, and re-layouts  3.65 us (3%)
    pallas_call x1, Pallas kernels, direct(): pl.pallas_call(lambda *refs: main_kernel(rows, cols, width, *refs), out_s...  129 us
    unnamed x6, local copies, waits for them, and re-layouts  3.65 us

profile of v4, /device:TPU:0, one launch (start us, length us, event | category | flops | bytes accessed | tf_op | source)
XLA Modules:
  0.0 133.5 jit_solution(9306427291521040020)
XLA Ops:
  0.6 0.0 copy-start
  0.6 1.1 copy-done
  1.8 0.0 copy-start.1
  1.8 0.9 copy-done.1
  2.7 129.2 %shard_map.41 = (f32[128,256]{1,0:T(8,128)S(1)}, f32[8,96,128]{2,1,0:T(8,128)S(1)}) custom-call(f32[256,256]{1,0:T(8,128)S(1)} %copy-done.1, f32[8,96,256]{2,1,0:T(8,128)S(1)} %bitcast.4), custom_call_target="tpu_custom_call" | custom-call | tf_op jit(solution)/shard_map/pallas_call | solution.py:387
  131.9 0.9 copy.4
  132.8 0.7 copy.6
Async XLA Ops:
  0.6 1.1 copy-start
  1.8 0.9 copy-start.1

commit v5 on v4

--- a/solution.py
+++ b/solution.py
@@ -289,33 +289,31 @@
     reduction.drain()
 
 
-def solve(cross_ref, inverse_ref, middle_ref, slab_ref):
+def solve(rows, cross_ref, inverse_ref, middle_ref, slab_ref, out_ref, send, receive):
+    row, col = lax.axis_index("row"), lax.axis_index("col")
     total = inverse_ref.shape[0]
     step = 2 * BLOCK
     for j in range(0, total, step):
         stop = j + step
         middle_ref[:, j:stop] = contract(cross_ref[:, :stop], inverse_ref[j:stop, :stop], 1, 1)
-    wide = total // slab_ref.shape[0]
-    for j in range(0, total, step):
+    wide = total // rows
+
+    def copy_to(peer):
+        s = lax.rem(peer - row + rows, rows)
+        return remote(slab_ref.at[peer], out_ref.at[row], send.at[s], receive.at[s], peer, col)
+
+    for j in range(total - step, -1, -step):
         found = contract(middle_ref[:, j:], inverse_ref[j:, j : j + step], 1, 0)
         for t in range(0, step, wide):
-            slab_ref[(j + t) // wide] = found[:, t : t + wide]
-
-
-def spread_slab(rows, slab_ref, out_ref, send, receive):
-    row, col = lax.axis_index("row"), lax.axis_index("col")
-    sent = []
-    for s in range(1, rows):
-        peer = lax.rem(row + s, rows)
-        copy = remote(slab_ref.at[peer], out_ref.at[row], send.at[s], receive.at[s], peer, col)
-        copy.start()
-        sent.append(copy)
+            peer = (j + t) // wide
+            slab_ref[peer] = found[:, t : t + wide]
+            pl.when(row != peer)(lambda peer=peer: copy_to(peer).start())
     out_ref[row] = slab_ref[row]
     for s in range(1, rows):
         place = out_ref.at[lax.rem(row - s + rows, rows)]
         remote(place, place, send.at[s], receive.at[s], lax.rem(row + s, rows), col).wait_recv()
-    for copy in sent:
-        copy.wait_send()
+    for s in range(1, rows):
+        copy_to(lax.rem(row + s, rows)).wait_send()
 
 
 def main_kernel(rows, cols, width, *refs):
@@ -354,8 +352,7 @@
         pl.ds(pl.multiple_of(col * upper_out.shape[1], BLOCK), upper_out.shape[1]),
     ]
     summed_ref[...] = wide.finish()
-    solve(summed_ref, inverse_ref, middle_ref, slab_ref)
-    spread_slab(rows, slab_ref, coef_out, *spreads)
+    solve(rows, summed_ref, inverse_ref, middle_ref, slab_ref, coef_out, *spreads)
     wide.drain()
 
 

time: 134 us -> 137 us (1.022)
  Pallas kernels: 129 us -> 132 us
    pallas_call x1, Pallas kernels: 129 us -> 132 us  [direct(): pl.pallas_call(lambda *refs: main_kernel(rows, cols, width, *refs), out_s...]
where the time goes in v5:
time: 137 us; the launch traced here: 136 us
  Pallas kernels  132 us (96%)
  local copies, waits for them, and re-layouts  3.65 us (3%)
    pallas_call x1, Pallas kernels, direct(): pl.pallas_call(lambda *refs: main_kernel(rows, cols, width, *refs), out_s...  132 us
    unnamed x6, local copies, waits for them, and re-layouts  3.65 us

profile of v5, /device:TPU:0, one launch (start us, length us, event | category | flops | bytes accessed | tf_op | source)
XLA Modules:
  0.0 136.4 jit_solution(16897958288240225168)
XLA Ops:
  0.6 0.0 copy-start
  0.6 1.1 copy-done
  1.8 0.0 copy-start.1
  1.8 0.9 copy-done.1
  2.7 132.1 %shard_map.41 = (f32[128,256]{1,0:T(8,128)S(1)}, f32[8,96,128]{2,1,0:T(8,128)S(1)}) custom-call(f32[256,256]{1,0:T(8,128)S(1)} %copy-done.1, f32[8,96,256]{2,1,0:T(8,128)S(1)} %bitcast.4), custom_call_target="tpu_custom_call" | custom-call | tf_op jit(solution)/shard_map/pallas_call | solution.py:384
  134.9 0.9 copy.4
  135.8 0.7 copy.6
Async XLA Ops:
  0.6 1.1 copy-start
  1.8 0.9 copy-start.1
